TPU v7x, 32 devices: a whole 2x2x4 slice. The times are simulated.
32 devices in a mesh: seg: 4 (over z), sec: 8 (over y, x, core).
Axes of the slice: x: 2, y: 2, z: 4, core: 2. Of those that a mesh axis runs over, the one named last changes fastest.
Arguments:
- start_vector: float32 [4, 1024, 2, 1024], P('seg', 'sec'), may hold values from -6 to 6
- left_env: bfloat16 [4, 5, 1024, 1024], P('seg', None, 'sec'), as said below
- right_env: bfloat16 [4, 5, 1024, 1024], P('seg', None, 'sec'), as said below
- charge_left: int32 [4, 1024], P('seg', 'sec'), may hold values from -8 to 8, as said below
- charge_right: int32 [4, 1024], P('seg'), may hold values from -8 to 8, as said below
Outputs:
- final_vector: float32 [4, 1024, 2, 1024], P('seg', 'sec')
- coefficients: float32 [4, 4], P('seg')
Inputs may be any that keep to these rules, and one draw needn't show every extreme that they name: `charge_left`: each segment's left bond holds both charges -8 and 8; charges gather near 0. `charge_right`: each segment's right bond holds both charges -8 and 8; charges gather near 0. left_env[g] is zero outside the charge rule stated for it, with the charges charge_left[(g + 1) mod 4]. right_env[g] is zero outside the charge rule stated for it, with the charges charge_right[(g - 1) mod 4].
All inputs are finite; a program needn't handle non-finite values.
Results may differ from a plain program's by a relative error of at most 0.0042.
Values may be sent and summed in bfloat16 or wider, within the bound.
A program may use at most 128 MiB of HBM per device.

v0:
```python
import jax
import jax.numpy as jnp
from jax import lax
from jax.sharding import PartitionSpec as P

CHI = 1024
ITERS = 4
EPS = 1e-06


def shifted(value, axis, steps):
    count = lax.axis_size(axis)
    pairs = [(source, (source + steps) % count) for source in range(count)]
    return lax.ppermute(value, axis, pairs)


def merged(env):
    return jnp.stack([env[0] + env[1] + env[2], env[3], env[4]])


def on_device(start_vector, left_env, right_env, charge_left, charge_right):
    left = shifted(merged(left_env[0]), "seg", 1)
    passed = shifted(merged(right_env[0]), "seg", -1)
    right = lax.all_gather(passed, "sec", axis=1, tiled=True)
    charges = charge_right[0]
    step = charges[None, :] - charges[:, None]
    right_stack = jnp.concatenate(
        [
            jnp.where(step == 0, right[0], 0),
            jnp.where(step == 1, right[0], 0),
            jnp.where(step == -1, right[0], 0),
            right[1],
            right[2],
        ],
        axis=0,
    )
    gap = charges[None, :] - charge_left[0][:, None]
    down, up = (gap == 0, gap == 1)
    allowed = down | up
    spin = jnp.where(up, 0.5, -0.5)
    rows = gap.shape[0]
    left_rows = left.reshape(3 * rows, left.shape[2])
    current = jnp.where(down, start_vector[0, :, 0], jnp.where(up, start_vector[0, :, 1], 0.0))
    norm = lax.psum(jnp.sum(current * current), "sec")
    current = current / jnp.sqrt(norm + EPS)
    previous = jnp.zeros_like(current)
    beta = jnp.float32(0.0)
    betas = []
    for _ in range(ITERS):
        whole = lax.all_gather(current.astype(jnp.bfloat16), "sec", axis=0, tiled=True)
        first = jnp.dot(left_rows, whole, preferred_element_type=jnp.float32)
        first = first.reshape(3, rows, -1)
        half = 0.5 * first[2]
        mixed = jnp.concatenate(
            [
                jnp.where(allowed, first[0] + spin * first[1], 0.0),
                jnp.where(up, half, 0.0),
                jnp.where(down, half, 0.0),
                jnp.where(allowed, spin * first[2], 0.0),
                jnp.where(allowed, first[2], 0.0),
            ],
            axis=1,
        ).astype(jnp.bfloat16)
        image = jnp.dot(mixed, right_stack, preferred_element_type=jnp.float32)
        residual = jnp.where(allowed, image, 0.0) - beta * previous
        alpha = lax.psum(jnp.sum(residual * current), "sec")
        residual = residual - alpha * current
        beta = jnp.sqrt(lax.psum(jnp.sum(residual * residual), "sec") + EPS)
        previous = current
        current = residual / beta
        betas.append(beta)
    scaled = current * CHI
    final = jnp.stack([jnp.where(down, scaled, 0.0), jnp.where(up, scaled, 0.0)], axis=1)
    return (final[None], jnp.stack(betas)[None])


def solution(mesh):
    return jax.shard_map(
        on_device,
        mesh=mesh,
        in_specs=(
            P("seg", "sec", None, None),
            P("seg", None, "sec", None),
            P("seg", None, "sec", None),
            P("seg", "sec"),
            P("seg", None),
        ),
        out_specs=(P("seg", "sec", None, None), P("seg", None)),
        check_vma=False,
    )
```

profile of v0, /device:TPU:0, one launch (start us, length us, event | category | flops | bytes accessed | tf_op | source)
XLA Modules:
  0.0 353.4 jit_solution(2616346199038595305)
XLA Ops:
  7.2 2.5 fusion.78
  10.7 15.8 %psum.63 = f32[]{:T(128)} all-reduce(f32[]{:T(128)} %multiply_reduce_fusion.8), channel_id=1, replica_groups=mesh['seg'=4,'sec'=8] {'sec'}, use_global_device_ids=true, to_apply=%region_1.2 | all-reduce | flops 1 | bytes 8 | tf_op jit(solution)/shard_map/psum | solution.py:44
  28.5 3.7 %collective-permute-start.1 = (bf16[3,128,1024]{2,1,0:T(8,128)(2,1)S(1)}, bf16[3,128,1024]{2,1,0:T(8,128)(2,1)S(1)}, u32[]{:S(2)}, u32[]{:S(2)}) collective-permute-start(bf16[3,128,1024]{2,1,0:T(8,128)(2,1)S(1)} %pad_maximum_fusion.1), channel_id=1, source_target_pairs={{0,24},{8,0},{16,8},{24,16},{1,25},{9,1},{17,9},{25,17},{2,26},{10... | collective-permute-start | bytes 2359304 | tf_op jit(solution)/shard_map/ppermute | solution.py:14
  32.1 16.1 %collective-permute-done.1 = bf16[3,128,1024]{2,1,0:T(8,128)(2,1)S(1)} collective-permute-done((bf16[3,128,1024]{2,1,0:T(8,128)(2,1)S(1)}, bf16[3,128,1024]{2,1,0:T(8,128)(2,1)S(1)}, u32[]{:S(2)}, u32[]{:S(2)}) %collective-permute-start.1) | collective-permute-done | bytes 786464 | tf_op jit(solution)/shard_map/ppermute | solution.py:14
  49.4 18.0 %collective-permute-done = bf16[3,128,1024]{2,1,0:T(8,128)(2,1)S(1)} collective-permute-done((bf16[3,128,1024]{2,1,0:T(8,128)(2,1)S(1)}, bf16[3,128,1024]{2,1,0:T(8,128)(2,1)S(1)}, u32[]{:S(2)}, u32[]{:S(2)}) %collective-permute-start) | collective-permute-done | bytes 786464 | tf_op jit(solution)/shard_map/ppermute | solution.py:14
  67.4 2.6 fusion.79
  70.8 32.6 %all-gather.8.cloned.1.call-done = bf16[3,1024,1024]{2,1,0:T(8,128)(2,1)} async-done(((bf16[3,128,1024]{2,1,0:T(8,128)(2,1)}), bf16[3,1024,1024]{2,1,0:T(8,128)(2,1)}) %all-gather.8.cloned.1.call-update) | async-done | bytes 6291472 | tf_op jit(solution)/shard_map/all_gather | solution.py:24
  103.4 2.4 fusion.5
  105.8 2.3 fusion.4
  109.2 2.8 multiply_reduce_fusion.7
  113.2 13.7 %psum.64 = f32[]{:T(128)} all-reduce(f32[]{:T(128)} %get-tuple-element.22), channel_id=1, replica_groups=mesh['seg'=4,'sec'=8] {'sec'}, use_global_device_ids=true, to_apply=%region_3.4 | all-reduce | flops 1 | bytes 8 | tf_op jit(solution)/shard_map/psum | solution.py:66
  126.9 1.4 multiply_reduce_fusion.6
  128.3 12.4 %psum.65 = f32[]{:T(128)} all-reduce(f32[]{:T(128)} %multiply_reduce_fusion.6), channel_id=1, replica_groups=mesh['seg'=4,'sec'=8] {'sec'}, use_global_device_ids=true, to_apply=%region_5.6 | all-reduce | flops 1 | bytes 8 | tf_op jit(solution)/shard_map/psum | solution.py:68
  141.4 1.5 fusion.76
  142.9 27.9 %all-gather.10.cloned.1.call-done = bf16[1024,1024]{1,0:T(8,128)(2,1)} async-done(((bf16[128,1024]{1,0:T(8,128)(2,1)}), bf16[1024,1024]{1,0:T(8,128)(2,1)}) %all-gather.10.cloned.1.call-update) | async-done | bytes 2097168 | tf_op jit(solution)/shard_map/all_gather | solution.py:50
  170.8 2.6 fusion.80
  174.2 6.3 %multiply_reduce_fusion.5 = (f32[]{:T(128)}, f32[128,1024]{1,0:T(8,128)S(1)}) fusion(f32[128,1024]{1,0:T(8,128)S(1)} %get-tuple-element.9, f32[128,1024]{1,0:T(8,128)S(1)} %get-tuple-element.11, f32[]{:T(128)} %sqrt.16, bf16[128,5120]{1,0:T(8,128)(2,1)S(1)} %fusion.55, bf16[5120,1024]{1,0:T(8,128)(2,1)} %copy-done, s32[128]{0:T(128)S(1)} %bitcast.120, ...), kind=kOutput, calls=%fused_computation.90 | convolution fusion | flops 1343356928 | bytes 13373960 | tf_op jit(solution)/shard_map/dot_general | solution.py:64
  180.6 13.7 %psum.66 = f32[]{:T(128)} all-reduce(f32[]{:T(128)} %get-tuple-element.24), channel_id=1, replica_groups=mesh['seg'=4,'sec'=8] {'sec'}, use_global_device_ids=true, to_apply=%region_7.8 | all-reduce | flops 1 | bytes 8 | tf_op jit(solution)/shard_map/psum | solution.py:66
  195.7 12.4 %psum.67 = f32[]{:T(128)} all-reduce(f32[]{:T(128)} %multiply_reduce_fusion.4), channel_id=1, replica_groups=mesh['seg'=4,'sec'=8] {'sec'}, use_global_device_ids=true, to_apply=%region_9.10 | all-reduce | flops 1 | bytes 8 | tf_op jit(solution)/shard_map/psum | solution.py:68
  208.8 1.5 fusion.75
  210.5 27.7 %all-gather.12.cloned.1.call-done = bf16[1024,1024]{1,0:T(8,128)(2,1)} async-done(((bf16[128,1024]{1,0:T(8,128)(2,1)}), bf16[1024,1024]{1,0:T(8,128)(2,1)}) %all-gather.12.cloned.1.call-update) | async-done | bytes 2097168 | tf_op jit(solution)/shard_map/all_gather | solution.py:50
  238.2 2.6 fusion.81
  241.6 6.3 %multiply_reduce_fusion.3 = (f32[]{:T(128)}, f32[128,1024]{1,0:T(8,128)S(1)}) fusion(f32[128,1024]{1,0:T(8,128)S(1)} %get-tuple-element.7, f32[128,1024]{1,0:T(8,128)S(1)} %get-tuple-element.9, f32[]{:T(128)} %sqrt.17, bf16[128,5120]{1,0:T(8,128)(2,1)S(1)} %fusion.56, bf16[5120,1024]{1,0:T(8,128)(2,1)} %copy-done, s32[128]{0:T(128)S(1)} %bitcast.126, ...), kind=kOutput, calls=%fused_computation.86 | convolution fusion | flops 1343356928 | bytes 13373960 | tf_op jit(solution)/shard_map/dot_general | solution.py:64
  248.0 13.7 %psum.68 = f32[]{:T(128)} all-reduce(f32[]{:T(128)} %get-tuple-element.26), channel_id=1, replica_groups=mesh['seg'=4,'sec'=8] {'sec'}, use_global_device_ids=true, to_apply=%region_11.12 | all-reduce | flops 1 | bytes 8 | tf_op jit(solution)/shard_map/psum | solution.py:66
  263.1 12.4 %psum.69 = f32[]{:T(128)} all-reduce(f32[]{:T(128)} %multiply_reduce_fusion.2), channel_id=1, replica_groups=mesh['seg'=4,'sec'=8] {'sec'}, use_global_device_ids=true, to_apply=%region_13.14 | all-reduce | flops 1 | bytes 8 | tf_op jit(solution)/shard_map/psum | solution.py:68
  276.2 1.5 fusion.74
  277.6 27.9 %all-gather.14.cloned.1.call-done = bf16[1024,1024]{1,0:T(8,128)(2,1)} async-done(((bf16[128,1024]{1,0:T(8,128)(2,1)}), bf16[1024,1024]{1,0:T(8,128)(2,1)}) %all-gather.14.cloned.1.call-update) | async-done | bytes 2097168 | tf_op jit(solution)/shard_map/all_gather | solution.py:50
  305.6 2.6 fusion.82
  309.0 6.3 %multiply_reduce_fusion.1 = (f32[]{:T(128)}, f32[128,1024]{1,0:T(8,128)S(1)}) fusion(f32[128,1024]{1,0:T(8,128)S(1)} %get-tuple-element.5, f32[128,1024]{1,0:T(8,128)S(1)} %get-tuple-element.7, f32[]{:T(128)} %sqrt.18, bf16[128,5120]{1,0:T(8,128)(2,1)S(1)} %fusion.57, bf16[5120,1024]{1,0:T(8,128)(2,1)} %copy-done, s32[128]{0:T(128)S(1)} %bitcast.132, ...), kind=kOutput, calls=%fused_computation.82 | convolution fusion | flops 1343356928 | bytes 13373960 | tf_op jit(solution)/shard_map/dot_general | solution.py:64
  315.4 13.7 %psum.70 = f32[]{:T(128)} all-reduce(f32[]{:T(128)} %get-tuple-element.28), channel_id=1, replica_groups=mesh['seg'=4,'sec'=8] {'sec'}, use_global_device_ids=true, to_apply=%region_15.16 | all-reduce | flops 1 | bytes 8 | tf_op jit(solution)/shard_map/psum | solution.py:66
  330.4 12.4 %psum.71 = f32[]{:T(128)} all-reduce(f32[]{:T(128)} %multiply_reduce_fusion), channel_id=1, replica_groups=mesh['seg'=4,'sec'=8] {'sec'}, use_global_device_ids=true, to_apply=%region_17.18 | all-reduce | flops 1 | bytes 8 | tf_op jit(solution)/shard_map/psum | solution.py:68
  344.5 1.8 copy.9
  (61 shorter events, 14.9 us)
Async XLA Ops:
  7.2 2.6 copy-start.2
  7.2 2.6 copy-start.6
  7.2 60.2 %all-gather.6.cloned.1.call-start = ((), (), s32[]{:S(2)}) async-start(), calls=%async_computation | async-start | bytes 2359296 | tf_op jit(solution)/shard_map/all_gather | solution.py:50
  9.8 18.5 %copy-start.3 = (bf16[1,5,128,1024]{3,2,1,0:T(8,128)(2,1)S(1)}, bf16[1,5,128,1024]{3,2,1,0:T(8,128)(2,1)}, u32[]{:S(2)}) copy-start(bf16[1,5,128,1024]{3,2,1,0:T(8,128)(2,1)} %param.7) | copy-start | bytes 3932164
  28.2 75.2 %all-gather.8.cloned.1.call-start = ((), (), s32[]{:S(2)}) async-start(), calls=%async_computation.1 | async-start | bytes 7077888 | tf_op jit(solution)/shard_map/all_gather | solution.py:24
  28.4 20.8 %copy-start.4 = (bf16[1,5,128,1024]{3,2,1,0:T(8,128)(2,1)S(1)}, bf16[1,5,128,1024]{3,2,1,0:T(8,128)(2,1)}, u32[]{:S(2)}) copy-start(bf16[1,5,128,1024]{3,2,1,0:T(8,128)(2,1)} %param.6) | copy-start | bytes 3932164
  28.5 19.7 %collective-permute-start.1 = (bf16[3,128,1024]{2,1,0:T(8,128)(2,1)S(1)}, bf16[3,128,1024]{2,1,0:T(8,128)(2,1)S(1)}, u32[]{:S(2)}, u32[]{:S(2)}) collective-permute-start(bf16[3,128,1024]{2,1,0:T(8,128)(2,1)S(1)} %pad_maximum_fusion.1), channel_id=1, source_target_pairs={{0,24},{8,0},{16,8},{24,16},{1,25},{9,1},{17,9},{25,17},{2,26},{10... | collective-permute-start | bytes 2359304 | tf_op jit(solution)/shard_map/ppermute | solution.py:14
  48.2 0.9 copy-start.5
  49.1 121.7 %all-gather.10.cloned.1.call-start = ((), (), s32[]{:S(2)}) async-start(), calls=%async_computation.2 | async-start | bytes 2359296 | tf_op jit(solution)/shard_map/all_gather | solution.py:50
  49.3 18.1 %collective-permute-start = (bf16[3,128,1024]{2,1,0:T(8,128)(2,1)S(1)}, bf16[3,128,1024]{2,1,0:T(8,128)(2,1)S(1)}, u32[]{:S(2)}, u32[]{:S(2)}) collective-permute-start(bf16[3,128,1024]{2,1,0:T(8,128)(2,1)S(1)} %pad_maximum_fusion), channel_id=1, source_target_pairs={{0,8},{8,16},{16,24},{24,0},{1,9},{9,17},{17,25},{25,1},{2,10},{10... | collective-permute-start | bytes 2359304 | tf_op jit(solution)/shard_map/ppermute | solution.py:14
  103.4 4.7 %copy-start.1 = (bf16[3,1024,1024]{2,1,0:T(8,128)(2,1)S(1)}, bf16[3,1024,1024]{2,1,0:T(8,128)(2,1)}, u32[]{:S(2)}) copy-start(bf16[3,1024,1024]{2,1,0:T(8,128)(2,1)} %all-gather.8.cloned.1.call-done) | copy-start | bytes 18874372
  109.2 4.0 %copy-start = (bf16[5120,1024]{1,0:T(8,128)(2,1)}, bf16[5120,1024]{1,0:T(8,128)(2,1)S(1)}, u32[]{:S(2)}) copy-start(bf16[5120,1024]{1,0:T(8,128)(2,1)S(1)} %fusion.6) | copy-start | bytes 31457284
  142.9 95.3 %all-gather.12.cloned.1.call-start = ((), (), s32[]{:S(2)}) async-start(), calls=%async_computation.3 | async-start | bytes 2359296 | tf_op jit(solution)/shard_map/all_gather | solution.py:50
  210.3 95.3 %all-gather.14.cloned.1.call-start = ((), (), s32[]{:S(2)}) async-start(), calls=%async_computation.4 | async-start | bytes 2359296 | tf_op jit(solution)/shard_map/all_gather | solution.py:50
Sparse Core Ops, SparseCore 0:
  28.3 27.1 all-gather.5
  58.0 45.3 all-gather.7
  143.0 27.7 all-gather.9
  210.4 27.7 all-gather.11
  277.8 27.7 all-gather.13
where the time goes:
time: 354 us; the launch traced here: 353 us
  waiting for transfers between devices  150 us (42%)
  blocking collectives  120 us (34%)
  matrix products  32.1 us (9%)
  other arithmetic  22.3 us (6%)
  between operations  17.6 us (5%)
  local copies, waits for them, and re-layouts  6.75 us (2%)
  starting transfers between devices  4.1 us (1%)
    all_gather x4, waiting for transfers between devices, on_device(): lax.all_gather(current.astype(jnp.bfloat16), 'sec', axis=0, tiled=True)  83.5 us
    psum x4, blocking collectives, on_device(): alpha = lax.psum(jnp.sum(residual * current), 'sec')  54.8 us
    psum x4, blocking collectives, on_device(): beta = jnp.sqrt(lax.psum(jnp.sum(residual * residual), 'sec') + EPS)  49.6 us
    ppermute x2, waiting for transfers between devices, shifted(): return lax.ppermute(value, axis, pairs)  34.1 us
    all_gather x1, waiting for transfers between devices, on_device(): right = lax.all_gather(passed, 'sec', axis=1, tiled=True)  32.6 us
    dot_general x4, matrix products, on_device(): image = jnp.dot(mixed, right_stack, preferred_element_type=jnp.float32)  21.8 us
    psum x1, blocking collectives, on_device(): norm = lax.psum(jnp.sum(current * current), 'sec')  15.8 us
    dot_general x4, matrix products, on_device(): first = jnp.dot(left_rows, whole, preferred_element_type=jnp.float32)  10.3 us
  transfers between devices with their start and end apart: 7, of which 6 were waited for; matrix products, arithmetic and copies ran while one was open for 1% of the time, Pallas kernels for 0%

commit v1 on v0

--- a/solution.py
+++ b/solution.py
@@ -21,7 +21,13 @@
 def on_device(start_vector, left_env, right_env, charge_left, charge_right):
     left = shifted(merged(left_env[0]), "seg", 1)
     passed = shifted(merged(right_env[0]), "seg", -1)
-    right = lax.all_gather(passed, "sec", axis=1, tiled=True)
+
+    def change_target_up(on_dim, target):
+        part_now = lax.all_gather(target, "sec")
+        o_now = jnp.concatenate(part_now, on_dim)
+        return o_now
+
+    right = change_target_up(1, passed)
     charges = charge_right[0]
     step = charges[None, :] - charges[:, None]
     right_stack = jnp.concatenate(

time: 354 us -> 355 us (level)
  local copies, waits for them, and re-layouts: 6.75 us -> 10.7 us
    slice x0 -> x1, local copies, waits for them, and re-layouts: none -> 3.93 us  [on_device(): right[2]]
where the time goes in v1:
time: 355 us; the launch traced here: 354 us
  waiting for transfers between devices  150 us (42%)
  blocking collectives  120 us (34%)
  matrix products  32.1 us (9%)
  other arithmetic  19 us (5%)
  between operations  17.6 us (5%)
  local copies, waits for them, and re-layouts  10.7 us (3%)
  starting transfers between devices  4.1 us (1%)
    all_gather x4, waiting for transfers between devices, on_device(): lax.all_gather(current.astype(jnp.bfloat16), 'sec', axis=0, tiled=True)  83.5 us
    psum x4, blocking collectives, on_device(): alpha = lax.psum(jnp.sum(residual * current), 'sec')  54.8 us
    psum x4, blocking collectives, on_device(): beta = jnp.sqrt(lax.psum(jnp.sum(residual * residual), 'sec') + EPS)  49.6 us
    ppermute x2, waiting for transfers between devices, shifted(): return lax.ppermute(value, axis, pairs)  34.1 us
    all_gather x1, waiting for transfers between devices, change_target_up(): part_now = lax.all_gather(target, 'sec')  32.6 us
    dot_general x4, matrix products, on_device(): image = jnp.dot(mixed, right_stack, preferred_element_type=jnp.float32)  21.8 us
    psum x1, blocking collectives, on_device(): norm = lax.psum(jnp.sum(current * current), 'sec')  15.8 us
    dot_general x4, matrix products, on_device(): first = jnp.dot(left_rows, whole, preferred_element_type=jnp.float32)  10.3 us
  transfers between devices with their start and end apart: 7, of which 6 were waited for; matrix products, arithmetic and copies ran while one was open for 1% of the time, Pallas kernels for 0%

profile of v1, /device:TPU:0, one launch (start us, length us, event | category | flops | bytes accessed | tf_op | source)
XLA Modules:
  0.0 353.9 jit_solution(15007221326425469855)
XLA Ops:
  7.2 2.5 fusion.77
  10.7 15.8 %psum.63 = f32[]{:T(128)} all-reduce(f32[]{:T(128)} %multiply_reduce_fusion.8), channel_id=1, replica_groups=mesh['seg'=4,'sec'=8] {'sec'}, use_global_device_ids=true, to_apply=%region_1.2 | all-reduce | flops 1 | bytes 8 | tf_op jit(solution)/shard_map/psum | solution.py:50
  28.5 3.7 %collective-permute-start.1 = (bf16[3,128,1024]{2,1,0:T(8,128)(2,1)S(1)}, bf16[3,128,1024]{2,1,0:T(8,128)(2,1)S(1)}, u32[]{:S(2)}, u32[]{:S(2)}) collective-permute-start(bf16[3,128,1024]{2,1,0:T(8,128)(2,1)S(1)} %pad_maximum_fusion.1), channel_id=1, source_target_pairs={{0,24},{8,0},{16,8},{24,16},{1,25},{9,1},{17,9},{25,17},{2,26},{10... | collective-permute-start | bytes 2359304 | tf_op jit(solution)/shard_map/ppermute | solution.py:14
  32.1 16.1 %collective-permute-done.1 = bf16[3,128,1024]{2,1,0:T(8,128)(2,1)S(1)} collective-permute-done((bf16[3,128,1024]{2,1,0:T(8,128)(2,1)S(1)}, bf16[3,128,1024]{2,1,0:T(8,128)(2,1)S(1)}, u32[]{:S(2)}, u32[]{:S(2)}) %collective-permute-start.1) | collective-permute-done | bytes 786464 | tf_op jit(solution)/shard_map/ppermute | solution.py:14
  49.4 18.0 %collective-permute-done = bf16[3,128,1024]{2,1,0:T(8,128)(2,1)S(1)} collective-permute-done((bf16[3,128,1024]{2,1,0:T(8,128)(2,1)S(1)}, bf16[3,128,1024]{2,1,0:T(8,128)(2,1)S(1)}, u32[]{:S(2)}, u32[]{:S(2)}) %collective-permute-start) | collective-permute-done | bytes 786464 | tf_op jit(solution)/shard_map/ppermute | solution.py:14
  67.4 2.6 fusion.78
  70.8 32.6 %all-gather.15.cloned.1.call-done = bf16[24,128,1024]{2,1,0:T(8,128)(2,1)} async-done(((bf16[3,128,1024]{2,1,0:T(8,128)(2,1)}), bf16[24,128,1024]{2,1,0:T(8,128)(2,1)}) %all-gather.15.cloned.1.call-update) | async-done | bytes 6291472 | tf_op jit(solution)/shard_map/all_gather | solution.py:26
  103.4 3.9 %fusion.76 = (bf16[1,8,128,1024]{3,2,0,1:T(8,128)(2,1)S(1)}, bf16[1,8,128,1024]{3,2,0,1:T(8,128)(2,1)S(1)}, bf16[1,8,128,1024]{3,2,0,1:T(8,128)(2,1)S(1)}) fusion(bf16[3,8,128,1024]{3,2,0,1:T(8,128)(2,1)} %bitcast.72), kind=kLoop, calls=%fused_computation.129 | loop fusion | bytes 12582912 | tf_op jit(solution)/shard_map/slice | solution.py:39
  109.8 2.8 multiply_reduce_fusion.7
  113.7 13.7 %psum.64 = f32[]{:T(128)} all-reduce(f32[]{:T(128)} %get-tuple-element.27), channel_id=1, replica_groups=mesh['seg'=4,'sec'=8] {'sec'}, use_global_device_ids=true, to_apply=%region_3.4 | all-reduce | flops 1 | bytes 8 | tf_op jit(solution)/shard_map/psum | solution.py:72
  128.8 12.4 %psum.65 = f32[]{:T(128)} all-reduce(f32[]{:T(128)} %multiply_reduce_fusion.6), channel_id=1, replica_groups=mesh['seg'=4,'sec'=8] {'sec'}, use_global_device_ids=true, to_apply=%region_5.6 | all-reduce | flops 1 | bytes 8 | tf_op jit(solution)/shard_map/psum | solution.py:74
  142.0 1.5 fusion.74
  143.7 27.7 %all-gather.9.cloned.1.call-done = bf16[1024,1024]{1,0:T(8,128)(2,1)} async-done(((bf16[128,1024]{1,0:T(8,128)(2,1)}), bf16[1024,1024]{1,0:T(8,128)(2,1)}) %all-gather.9.cloned.1.call-update) | async-done | bytes 2097168 | tf_op jit(solution)/shard_map/all_gather | solution.py:56
  171.4 2.6 fusion.79
  174.8 6.3 %multiply_reduce_fusion.5 = (f32[]{:T(128)}, f32[128,1024]{1,0:T(8,128)S(1)}) fusion(f32[128,1024]{1,0:T(8,128)S(1)} %get-tuple-element.11, f32[128,1024]{1,0:T(8,128)S(1)} %get-tuple-element.13, f32[]{:T(128)} %sqrt.16, bf16[128,5120]{1,0:T(8,128)(2,1)S(1)} %fusion.53, bf16[5120,1024]{1,0:T(8,128)(2,1)} %copy-done, s32[128]{0:T(128)S(1)} %bitcast.116, ...), kind=kOutput, calls=%fused_computation.85 | convolution fusion | flops 1343356928 | bytes 13373960 | tf_op jit(solution)/shard_map/dot_general | solution.py:70
  181.1 13.7 %psum.66 = f32[]{:T(128)} all-reduce(f32[]{:T(128)} %get-tuple-element.29), channel_id=1, replica_groups=mesh['seg'=4,'sec'=8] {'sec'}, use_global_device_ids=true, to_apply=%region_7.8 | all-reduce | flops 1 | bytes 8 | tf_op jit(solution)/shard_map/psum | solution.py:72
  194.8 1.4 multiply_reduce_fusion.4
  196.2 12.4 %psum.67 = f32[]{:T(128)} all-reduce(f32[]{:T(128)} %multiply_reduce_fusion.4), channel_id=1, replica_groups=mesh['seg'=4,'sec'=8] {'sec'}, use_global_device_ids=true, to_apply=%region_9.10 | all-reduce | flops 1 | bytes 8 | tf_op jit(solution)/shard_map/psum | solution.py:74
  209.3 1.5 fusion.73
  210.9 27.9 %all-gather.11.cloned.1.call-done = bf16[1024,1024]{1,0:T(8,128)(2,1)} async-done(((bf16[128,1024]{1,0:T(8,128)(2,1)}), bf16[1024,1024]{1,0:T(8,128)(2,1)}) %all-gather.11.cloned.1.call-update) | async-done | bytes 2097168 | tf_op jit(solution)/shard_map/all_gather | solution.py:56
  238.8 2.6 fusion.80
  242.2 6.3 %multiply_reduce_fusion.3 = (f32[]{:T(128)}, f32[128,1024]{1,0:T(8,128)S(1)}) fusion(f32[128,1024]{1,0:T(8,128)S(1)} %get-tuple-element.9, f32[128,1024]{1,0:T(8,128)S(1)} %get-tuple-element.11, f32[]{:T(128)} %sqrt.17, bf16[128,5120]{1,0:T(8,128)(2,1)S(1)} %fusion.54, bf16[5120,1024]{1,0:T(8,128)(2,1)} %copy-done, s32[128]{0:T(128)S(1)} %bitcast.122, ...), kind=kOutput, calls=%fused_computation.81 | convolution fusion | flops 1343356928 | bytes 13373960 | tf_op jit(solution)/shard_map/dot_general | solution.py:70
  248.5 13.7 %psum.68 = f32[]{:T(128)} all-reduce(f32[]{:T(128)} %get-tuple-element.31), channel_id=1, replica_groups=mesh['seg'=4,'sec'=8] {'sec'}, use_global_device_ids=true, to_apply=%region_11.12 | all-reduce | flops 1 | bytes 8 | tf_op jit(solution)/shard_map/psum | solution.py:72
  263.6 12.4 %psum.69 = f32[]{:T(128)} all-reduce(f32[]{:T(128)} %multiply_reduce_fusion.2), channel_id=1, replica_groups=mesh['seg'=4,'sec'=8] {'sec'}, use_global_device_ids=true, to_apply=%region_13.14 | all-reduce | flops 1 | bytes 8 | tf_op jit(solution)/shard_map/psum | solution.py:74
  276.7 1.5 fusion.72
  278.2 27.9 %all-gather.13.cloned.1.call-done = bf16[1024,1024]{1,0:T(8,128)(2,1)} async-done(((bf16[128,1024]{1,0:T(8,128)(2,1)}), bf16[1024,1024]{1,0:T(8,128)(2,1)}) %all-gather.13.cloned.1.call-update) | async-done | bytes 2097168 | tf_op jit(solution)/shard_map/all_gather | solution.py:56
  306.1 2.6 fusion.81
  309.6 6.3 %multiply_reduce_fusion.1 = (f32[]{:T(128)}, f32[128,1024]{1,0:T(8,128)S(1)}) fusion(f32[128,1024]{1,0:T(8,128)S(1)} %get-tuple-element.7, f32[128,1024]{1,0:T(8,128)S(1)} %get-tuple-element.9, f32[]{:T(128)} %sqrt.18, bf16[128,5120]{1,0:T(8,128)(2,1)S(1)} %fusion.55, bf16[5120,1024]{1,0:T(8,128)(2,1)} %copy-done, s32[128]{0:T(128)S(1)} %bitcast.128, ...), kind=kOutput, calls=%fused_computation.77 | convolution fusion | flops 1343356928 | bytes 13373960 | tf_op jit(solution)/shard_map/dot_general | solution.py:70
  315.9 13.7 %psum.70 = f32[]{:T(128)} all-reduce(f32[]{:T(128)} %get-tuple-element.33), channel_id=1, replica_groups=mesh['seg'=4,'sec'=8] {'sec'}, use_global_device_ids=true, to_apply=%region_15.16 | all-reduce | flops 1 | bytes 8 | tf_op jit(solution)/shard_map/psum | solution.py:72
  329.6 1.4 multiply_reduce_fusion
  331.0 12.4 %psum.71 = f32[]{:T(128)} all-reduce(f32[]{:T(128)} %multiply_reduce_fusion), channel_id=1, replica_groups=mesh['seg'=4,'sec'=8] {'sec'}, use_global_device_ids=true, to_apply=%region_17.18 | all-reduce | flops 1 | bytes 8 | tf_op jit(solution)/shard_map/psum | solution.py:74
  345.0 1.8 copy.12
  (60 shorter events, 14.8 us)
Async XLA Ops:
  7.2 2.6 copy-start.1
  7.2 2.6 copy-start.5
  7.2 60.2 %all-gather.7.cloned.1.call-start = ((), (), s32[]{:S(2)}) async-start(), calls=%async_computation | async-start | bytes 2359296 | tf_op jit(solution)/shard_map/all_gather | solution.py:56
  9.8 18.5 %copy-start.2 = (bf16[1,5,128,1024]{3,2,1,0:T(8,128)(2,1)S(1)}, bf16[1,5,128,1024]{3,2,1,0:T(8,128)(2,1)}, u32[]{:S(2)}) copy-start(bf16[1,5,128,1024]{3,2,1,0:T(8,128)(2,1)} %param.7) | copy-start | bytes 3932164
  28.2 75.2 %all-gather.15.cloned.1.call-start = ((), (), s32[]{:S(2)}) async-start(), calls=%async_computation.4 | async-start | bytes 7077888 | tf_op jit(solution)/shard_map/all_gather | solution.py:26
  28.4 20.8 %copy-start.3 = (bf16[1,5,128,1024]{3,2,1,0:T(8,128)(2,1)S(1)}, bf16[1,5,128,1024]{3,2,1,0:T(8,128)(2,1)}, u32[]{:S(2)}) copy-start(bf16[1,5,128,1024]{3,2,1,0:T(8,128)(2,1)} %param.6) | copy-start | bytes 3932164
  28.5 19.7 %collective-permute-start.1 = (bf16[3,128,1024]{2,1,0:T(8,128)(2,1)S(1)}, bf16[3,128,1024]{2,1,0:T(8,128)(2,1)S(1)}, u32[]{:S(2)}, u32[]{:S(2)}) collective-permute-start(bf16[3,128,1024]{2,1,0:T(8,128)(2,1)S(1)} %pad_maximum_fusion.1), channel_id=1, source_target_pairs={{0,24},{8,0},{16,8},{24,16},{1,25},{9,1},{17,9},{25,17},{2,26},{10... | collective-permute-start | bytes 2359304 | tf_op jit(solution)/shard_map/ppermute | solution.py:14
  48.2 0.9 copy-start.4
  49.1 122.3 %all-gather.9.cloned.1.call-start = ((), (), s32[]{:S(2)}) async-start(), calls=%async_computation.1 | async-start | bytes 2359296 | tf_op jit(solution)/shard_map/all_gather | solution.py:56
  49.3 18.1 %collective-permute-start = (bf16[3,128,1024]{2,1,0:T(8,128)(2,1)S(1)}, bf16[3,128,1024]{2,1,0:T(8,128)(2,1)S(1)}, u32[]{:S(2)}, u32[]{:S(2)}) collective-permute-start(bf16[3,128,1024]{2,1,0:T(8,128)(2,1)S(1)} %pad_maximum_fusion), channel_id=1, source_target_pairs={{0,8},{8,16},{16,24},{24,0},{1,9},{9,17},{17,25},{25,1},{2,10},{10... | collective-permute-start | bytes 2359304 | tf_op jit(solution)/shard_map/ppermute | solution.py:14
  109.8 4.0 %copy-start = (bf16[5120,1024]{1,0:T(8,128)(2,1)}, bf16[5120,1024]{1,0:T(8,128)(2,1)S(1)}, u32[]{:S(2)}) copy-start(bf16[5120,1024]{1,0:T(8,128)(2,1)S(1)} %constant_dynamic-update-slice_fusion) | copy-start | bytes 31457284
  143.4 95.3 %all-gather.11.cloned.1.call-start = ((), (), s32[]{:S(2)}) async-start(), calls=%async_computation.2 | async-start | bytes 2359296 | tf_op jit(solution)/shard_map/all_gather | solution.py:56
  210.8 95.3 %all-gather.13.cloned.1.call-start = ((), (), s32[]{:S(2)}) async-start(), calls=%async_computation.3 | async-start | bytes 2359296 | tf_op jit(solution)/shard_map/all_gather | solution.py:56
Sparse Core Ops, SparseCore 0:
  28.3 27.1 all-gather.6
  58.0 45.3 all-gather.14
  143.6 27.7 all-gather.8
  210.9 27.7 all-gather.10
  278.3 27.7 all-gather.12
